TPU v7x, 32 devices: a whole 2x2x4 slice. The times are simulated.
32 devices in a mesh: expert: 8 (over y, x, core), dp: 4 (over z).
Axes of the slice: x: 2, y: 2, z: 4, core: 2. Of those that a mesh axis runs over, the one named last changes fastest.
Arguments:
- trunk: bfloat16 [768, 4096], P(('dp', 'expert')), may hold values from -6 to 6
- w_first: bfloat16 [8, 4096, 2048], P('expert'), may hold values from -0.09375 to 0.09375
- w_second: bfloat16 [8, 2048, 1024], P('expert'), may hold values from -0.125 to 0.125
- gates: bfloat16 [8, 8, 768], P('expert', None, 'dp'), may hold values from 0.049804688 to 1
- d_mixed: bfloat16 [768, 8, 1024], P(('dp', 'expert')), may hold values from -6 to 6
Outputs:
- mixed: bfloat16 [768, 8, 1024], P(('dp', 'expert'))
- d_trunk: bfloat16 [768, 4096], P(('dp', 'expert'))
- d_gates: bfloat16 [8, 8, 768], P('expert', None, 'dp')
- d_w_first: bfloat16 [8, 4096, 2048], P('expert', 'dp')
- d_w_second: bfloat16 [8, 2048, 1024], P('expert', 'dp')
All inputs are finite; a program needn't handle non-finite values.
Results may differ from a plain program's by a relative error of at most 0.015.
Values may be sent and summed in bfloat16 or wider, within the bound.
A program may use at most 128 MiB of HBM per device.

v0:
```python
import jax
import jax.numpy as jnp
from jax import lax
from jax.sharding import PartitionSpec as P

F32 = jnp.float32
BF16 = jnp.bfloat16


def on_device(trunk, w_first, w_second, gates, d_mixed):
    rank = lax.axis_index("dp")
    first = w_first[0]
    second = w_second[0]
    gate_here = gates[0]
    n_dp = lax.axis_size("dp")
    depth = first.shape[0] // n_dp
    units = second.shape[0] // n_dp
    group = gate_here.shape[1]
    rows_all = lax.all_gather(trunk, ("dp", "expert"), axis=0, tiled=True)
    gates_each = lax.all_to_all(
        gate_here.T[None], "expert", split_axis=1, concat_axis=0, tiled=True
    )
    d_out_each = jnp.einsum("ert,rto->ero", gates_each, d_mixed, preferred_element_type=F32).astype(
        BF16
    )
    d_output = lax.all_to_all(d_out_each, "expert", split_axis=0, concat_axis=1, tiled=True)[0]
    d_output_all = lax.all_gather(d_output, "dp", axis=0, tiled=True)
    pre = jnp.dot(rows_all, first, preferred_element_type=F32)
    pre_here = lax.dynamic_slice_in_dim(pre, rank * group, group, 0)
    hidden_here = jax.nn.silu(pre_here).astype(BF16)
    output = jnp.dot(hidden_here, second, preferred_element_type=F32).astype(BF16)
    outs_each = lax.all_to_all(output[None], "expert", split_axis=1, concat_axis=0, tiled=True)
    d_hidden = lax.dot_general(
        d_output_all, second, (((1,), (1,)), ((), ())), preferred_element_type=F32
    )
    sig = jax.nn.sigmoid(pre)
    d_pre = (d_hidden * sig * (1.0 + pre * (1.0 - sig))).astype(BF16)
    d_pre_here = lax.dynamic_slice_in_dim(d_pre, rank * group, group, 0)
    d_trunk = lax.psum_scatter(
        lax.dot_general(
            d_pre_here, first, (((1,), (1,)), ((), ())), preferred_element_type=F32
        ).astype(BF16),
        "expert",
        scatter_dimension=0,
        tiled=True,
    )
    mixed = jnp.einsum("ert,ero->rto", gates_each, outs_each, preferred_element_type=F32).astype(
        BF16
    )
    d_gate_each = jnp.einsum("rto,ero->ert", d_mixed, outs_each, preferred_element_type=F32).astype(
        BF16
    )
    back_gate = lax.all_to_all(d_gate_each, "expert", split_axis=0, concat_axis=1, tiled=True)
    d_gate = back_gate[0].T[None]
    columns = lax.dynamic_slice_in_dim(rows_all, rank * depth, depth, 1)
    d_first = lax.dot_general(
        columns, d_pre, (((0,), (0,)), ((), ())), preferred_element_type=F32
    ).astype(BF16)
    some_pre = lax.dynamic_slice_in_dim(pre, rank * units, units, 1)
    some_hidden = jax.nn.silu(some_pre).astype(BF16)
    d_second = lax.dot_general(
        some_hidden, d_output_all, (((0,), (0,)), ((), ())), preferred_element_type=F32
    ).astype(BF16)
    return (mixed, d_trunk, d_gate, d_first[None], d_second[None])


def solution(mesh):
    in_specs = (
        P(("dp", "expert"), None),
        P("expert", None, None),
        P("expert", None, None),
        P("expert", None, "dp"),
        P(("dp", "expert"), None, None),
    )
    out_specs = (
        P(("dp", "expert"), None, None),
        P(("dp", "expert"), None),
        P("expert", None, "dp"),
        P("expert", "dp", None),
        P("expert", "dp", None),
    )
    return jax.shard_map(
        on_device, mesh=mesh, in_specs=in_specs, out_specs=out_specs, check_vma=False
    )
```

profile of v0, /device:TPU:0, one launch (start us, length us, event | category | flops | bytes accessed | tf_op | source)
XLA Modules:
  0.0 188.0 jit_solution(14458525638862660231)
XLA Ops:
  7.2 0.0 copy-start
  7.2 0.0 all-gather.3.cloned.1.call-start
  7.2 0.7 all-gather.3.cloned.1.call-update
  7.9 0.8 copy.28
  8.7 10.2 %all_to_all.42 = bf16[1,192,8]{2,0,1:T(2,128)(2,1)S(1)} all-to-all(bf16[1,192,8]{2,0,1:T(2,128)(2,1)S(1)} %copy.28), channel_id=1, replica_groups=mesh['expert'=8,'dp'=4] {'expert'}, dimensions={1} | all-to-all | bytes 6144 | tf_op jit(solution)/shard_map/all_to_all | solution.py:20
  18.9 0.1 copy.29
  19.0 0.1 all_to_all.15
  19.1 0.1 copy.32
  19.2 0.0 copy-done
  19.2 0.2 fusion.19
  19.5 1.0 copy.33
  20.5 3.5 %all-to-all-start.2 = ((bf16[8,24,1024]{2,1,0:T(8,128)(2,1)}), bf16[8,24,1024]{2,1,0:T(8,128)(2,1)S(1)}, u32[]{:S(2)}, u32[]{:S(2)}) async-start(bf16[8,24,1024]{2,1,0:T(8,128)(2,1)} %copy.33), calls=%async_computation.2 | async-start | bytes 786432 | tf_op jit(solution)/shard_map/all_to_all | solution.py:26
  23.9 0.0 all-gather.5.cloned.1.call-start
  24.0 8.2 %all-to-all-done.2 = bf16[8,24,1024]{2,1,0:T(8,128)(2,1)S(1)} async-done(((bf16[8,24,1024]{2,1,0:T(8,128)(2,1)}), bf16[8,24,1024]{2,1,0:T(8,128)(2,1)S(1)}, u32[]{:S(2)}, u32[]{:S(2)}) %all-to-all-start.2) | async-done | bytes 393248 | tf_op jit(solution)/shard_map/all_to_all | solution.py:26
  32.2 0.0 copy-start.1
  32.2 0.7 copy-done.1
  32.9 0.0 all-gather.5.cloned.1.call-update
  32.9 0.0 reduce-scatter.2.cloned.1.call-start
  33.0 49.8 %all-gather.3.cloned.1.call-done = bf16[768,4096]{1,0:T(8,128)(2,1)} async-done(((bf16[24,4096]{1,0:T(8,128)(2,1)}), bf16[768,4096]{1,0:T(8,128)(2,1)}) %all-gather.3.cloned.1.call-update) | async-done | bytes 6291472 | tf_op jit(solution)/shard_map/all_gather | solution.py:19
  82.8 20.2 %fusion.2 = f32[768,2048]{1,0:T(8,128)} fusion(bf16[768,4096]{1,0:T(8,128)(2,1)} %all-gather.3.cloned.1.call-done, bf16[1,4096,2048]{2,1,0:T(8,128)(2,1)} %param.6), kind=kOutput, calls=%fused_computation.2 | convolution fusion | flops 12884901888 | bytes 29360128 | tf_op jit(solution)/shard_map/dot_general | solution.py:28
  103.0 17.5 %all-gather.5.cloned.1.call-done = bf16[768,1024]{1,0:T(8,128)(2,1)} async-done(((bf16[192,1024]{1,0:T(8,128)(2,1)}), bf16[768,1024]{1,0:T(8,128)(2,1)}) %all-gather.5.cloned.1.call-update) | async-done | bytes 1572880 | tf_op jit(solution)/shard_map/all_gather | solution.py:27
  120.5 10.8 %multiply_convert_fusion = bf16[768,2048]{1,0:T(8,128)(2,1)} fusion(f32[768,2048]{1,0:T(8,128)} %fusion.2, bf16[768,1024]{1,0:T(8,128)(2,1)} %all-gather.5.cloned.1.call-done, bf16[1,2048,1024]{2,1,0:T(8,128)(2,1)} %param.7), kind=kOutput, calls=%fused_computation.4 | convolution fusion | flops 3235381248 | bytes 15204352 | tf_op jit(solution)/shard_map/dot_general | solution.py:33
  131.3 12.8 %fusion.4 = bf16[192,4096]{1,0:T(8,128)(2,1)} fusion(bf16[1,4096,2048]{2,1,0:T(8,128)(2,1)} %param.6, bf16[768,2048]{1,0:T(8,128)(2,1)} %multiply_convert_fusion, s32[]{:T(128)S(6)} %select_n.10), kind=kOutput, calls=%fused_computation.5 | convolution fusion | flops 3222011904 | bytes 19136516 | tf_op jit(solution)/shard_map/dot_general | solution.py:40
  144.1 0.0 reduce-scatter.2.cloned.1.call-update
  144.1 3.7 %fusion.20 = bf16[1,192,1024]{2,1,0:T(8,128)(2,1)S(1)} fusion(bf16[1,2048,1024]{2,1,0:T(8,128)(2,1)} %param.7, f32[768,2048]{1,0:T(8,128)} %fusion.2, s32[]{:T(128)S(6)} %select_n.10), kind=kOutput, calls=%fused_computation.21 | convolution fusion | flops 807469056 | bytes 6160388 | tf_op jit(solution)/shard_map/dot_general | solution.py:31
  147.8 0.6 copy.43
  148.4 0.5 broadcast.9
  148.9 2.9 %reduce = bf16[192,1024]{1,0:T(8,128)(2,1)S(1)} reduce(bf16[192,1,1024]{2,1,0:T(2,128)(2,1)S(1)} %bitcast.56, bf16[]{:T(256)} %broadcast.9), dimensions={1}, to_apply=%bitcast.55.reduce_sub_computation | reduce | bytes 786434
  151.9 1.2 reshape.24
  153.1 3.6 %all-to-all-start = ((bf16[8,2,12288]{2,1,0:T(2,128)(2,1)}), bf16[8,2,12288]{2,1,0:T(2,128)(2,1)S(1)}, u32[]{:S(2)}, u32[]{:S(2)}) async-start(bf16[8,2,12288]{2,1,0:T(2,128)(2,1)} %reshape.24), calls=%async_computation | async-start | bytes 786432 | tf_op jit(solution)/shard_map/all_to_all | solution.py:32
  156.7 0.0 copy-start.2
  156.7 8.0 %convert_bitcast_fusion = bf16[1,1024,2048]{2,1,0:T(8,128)(2,1)} fusion(bf16[768,2048]{1,0:T(8,128)(2,1)} %multiply_convert_fusion, bf16[768,4096]{1,0:T(8,128)(2,1)} %all-gather.3.cloned.1.call-done, s32[]{:T(128)S(6)} %select_n.11), kind=kOutput, calls=%fused_computation.10 | convolution fusion | flops 3223322624 | bytes 8912900 | tf_op jit(solution)/shard_map/dot_general | solution.py:56
  164.7 0.0 copy-done.2
  164.7 3.4 %fusion.14 = bf16[1,512,1024]{2,1,0:T(8,128)(2,1)} fusion(bf16[768,1024]{1,0:T(8,128)(2,1)S(1)} %copy-done.2, f32[768,2048]{1,0:T(8,128)} %fusion.2, s32[]{:T(128)S(6)} %select_n.12), kind=kOutput, calls=%fused_computation.15 | convolution fusion | flops 807796736 | bytes 4194308 | tf_op jit(solution)/shard_map/dot_general | solution.py:61
  168.2 0.0 all-to-all-done
  168.2 0.4 reshape.25
  168.6 0.1 copy.37
  168.7 0.4 fusion.23
  169.1 0.7 copy.35
  169.8 4.2 %all-to-all-start.3 = ((bf16[8,24,8]{1,2,0:T(8,128)(2,1)}), bf16[8,24,8]{1,2,0:T(8,128)(2,1)S(1)}, u32[]{:S(2)}, u32[]{:S(2)}) async-start(bf16[8,24,8]{1,2,0:T(8,128)(2,1)} %copy.35), calls=%async_computation.4 | async-start | bytes 32768 | tf_op jit(solution)/shard_map/all_to_all | solution.py:53
  174.0 1.1 fusion.18
  175.1 3.7 %all-to-all-done.3 = bf16[8,24,8]{1,2,0:T(8,128)(2,1)S(1)} async-done(((bf16[8,24,8]{1,2,0:T(8,128)(2,1)}), bf16[8,24,8]{1,2,0:T(8,128)(2,1)S(1)}, u32[]{:S(2)}, u32[]{:S(2)}) %all-to-all-start.3) | async-done | bytes 3104 | tf_op jit(solution)/shard_map/all_to_all | solution.py:53
  178.8 0.7 squeeze.19
  179.5 2.0 %reduce-scatter.2.cloned.1.call-done = bf16[24,4096]{1,0:T(8,128)(2,1)} async-done(((bf16[192,4096]{1,0:T(8,128)(2,1)}), bf16[24,4096]{1,0:T(8,128)(2,1)}) %reduce-scatter.2.cloned.1.call-update) | async-done | bytes 196624 | tf_op jit(solution)/shard_map/reduce_scatter | solution.py:39
  (1 shorter events, 0.0 us)
Async XLA Ops:
  7.2 12.1 %copy-start = (bf16[24,8,1024]{2,1,0:T(8,128)(2,1)S(1)}, bf16[24,8,1024]{2,1,0:T(8,128)(2,1)}, u32[]{:S(2)}) copy-start(bf16[24,8,1024]{2,1,0:T(8,128)(2,1)} %param.9) | copy-start | bytes 1179652
  7.2 75.6 %all-gather.3.cloned.1.call-start = ((), (), s32[]{:S(2)}) async-start(), calls=%async_computation.5 | async-start | bytes 6488064 | tf_op jit(solution)/shard_map/all_gather | solution.py:19
  20.5 11.7 %all-to-all-start.2 = ((bf16[8,24,1024]{2,1,0:T(8,128)(2,1)}), bf16[8,24,1024]{2,1,0:T(8,128)(2,1)S(1)}, u32[]{:S(2)}, u32[]{:S(2)}) async-start(bf16[8,24,1024]{2,1,0:T(8,128)(2,1)} %copy.33), calls=%async_computation.2 | async-start | bytes 786432 | tf_op jit(solution)/shard_map/all_to_all | solution.py:26
  23.9 96.6 %all-gather.5.cloned.1.call-start = ((), (), s32[]{:S(2)}) async-start(), calls=%async_computation.6 | async-start | bytes 1966080 | tf_op jit(solution)/shard_map/all_gather | solution.py:27
  32.2 0.7 copy-start.1
  32.9 148.6 %reduce-scatter.2.cloned.1.call-start = ((), (), s32[]{:S(2)}) async-start(), calls=%async_computation.7 | async-start | bytes 1769472 | tf_op jit(solution)/shard_map/reduce_scatter | solution.py:39
  153.1 15.1 %all-to-all-start = ((bf16[8,2,12288]{2,1,0:T(2,128)(2,1)}), bf16[8,2,12288]{2,1,0:T(2,128)(2,1)S(1)}, u32[]{:S(2)}, u32[]{:S(2)}) async-start(bf16[8,2,12288]{2,1,0:T(2,128)(2,1)} %reshape.24), calls=%async_computation | async-start | bytes 786432 | tf_op jit(solution)/shard_map/all_to_all | solution.py:32
  156.7 8.0 %copy-start.2 = (bf16[768,1024]{1,0:T(8,128)(2,1)S(1)}, bf16[768,1024]{1,0:T(8,128)(2,1)}, u32[]{:S(2)}) copy-start(bf16[768,1024]{1,0:T(8,128)(2,1)} %all-gather.5.cloned.1.call-done) | copy-start | bytes 4718596
  169.8 9.0 %all-to-all-start.3 = ((bf16[8,24,8]{1,2,0:T(8,128)(2,1)}), bf16[8,24,8]{1,2,0:T(8,128)(2,1)S(1)}, u32[]{:S(2)}, u32[]{:S(2)}) async-start(bf16[8,24,8]{1,2,0:T(8,128)(2,1)} %copy.35), calls=%async_computation.4 | async-start | bytes 32768 | tf_op jit(solution)/shard_map/all_to_all | solution.py:53
Sparse Core Ops, SparseCore 0:
  10.9 71.8 all-gather.2
  84.9 35.5 all-gather.4
  144.2 37.2 reduce-scatter.1
where the time goes:
time: 189 us; the launch traced here: 188 us
  waiting for transfers between devices  81.9 us (43%)
  matrix products  60.7 us (32%)
  between operations  13.8 us (7%)
  starting transfers between devices  11.4 us (6%)
  blocking collectives  10.2 us (5%)
  local copies, waits for them, and re-layouts  7.07 us (4%)
  other arithmetic  2.92 us (2%)
    all_gather x1, waiting for transfers between devices, on_device(): rows_all = lax.all_gather(trunk, ('dp', 'expert'), axis=0, tiled=True)  49.8 us
    dot_general x1, matrix products, on_device(): pre = jnp.dot(rows_all, first, preferred_element_type=F32)  20.2 us
    all_gather x1, waiting for transfers between devices, on_device(): d_output_all = lax.all_gather(d_output, 'dp', axis=0, tiled=True)  17.5 us
    dot_general x1, matrix products, on_device(): lax.dot_general(d_pre_here, first, (((1,), (1,)), ((), ())), preferred_el...  12.8 us
    dot_general x1, matrix products, on_device(): lax.dot_general(d_output_all, second, (((1,), (1,)), ((), ())), preferred...  10.8 us
    all_to_all x1, blocking collectives, on_device(): lax.all_to_all(gate_here.T[None], 'expert', split_axis=1, concat_axis=0,...  10.2 us
    all_to_all x1, waiting for transfers between devices, on_device(): lax.all_to_all(d_out_each, 'expert', split_axis=0, concat_axis=1, tiled=T...  8.19 us
    dot_general x1, matrix products, on_device(): lax.dot_general(columns, d_pre, (((0,), (0,)), ((), ())), preferred_eleme...  7.99 us
  transfers between devices with their start and end apart: 6, of which 5 were waited for; matrix products, arithmetic and copies ran while one was open for 25% of the time, Pallas kernels for 0%

commit v1 on v0

--- a/solution.py
+++ b/solution.py
@@ -16,7 +16,10 @@
     depth = first.shape[0] // n_dp
     units = second.shape[0] // n_dp
     group = gate_here.shape[1]
-    rows_all = lax.all_gather(trunk, ("dp", "expert"), axis=0, tiled=True)
+    oldest = lax.psum(1, ("dp", "expert"))
+    reached = jnp.stack(oldest * [trunk])
+    fresh = lax.all_to_all(reached, ("dp", "expert"), 0, 0)
+    rows_all = jnp.concatenate(fresh, 0)
     gates_each = lax.all_to_all(
         gate_here.T[None], "expert", split_axis=1, concat_axis=0, tiled=True
     )

time: 189 us -> 291 us (1.54)
  waiting for transfers between devices: 81.9 us -> 170 us
  blocking collectives: 10.2 us -> 21.6 us
    all_to_all x1, waiting for transfers between devices: 8.19 us -> 163 us  [on_device(): fresh = lax.all_to_all(reached, ('dp', 'expert'), 0, 0)]
    all_gather x1 -> x0, waiting for transfers between devices: 49.8 us -> none  [on_device(): rows_all = lax.all_gather(trunk, ('dp', 'expert'), axis=0, tiled=True)]
    all_gather x1, waiting for transfers between devices: 17.5 us -> 0.01 us  [on_device(): d_output_all = lax.all_gather(d_output, 'dp', axis=0, tiled=True)]
    all_to_all x0 -> x1, blocking collectives: none -> 11.4 us  [on_device(): lax.all_to_all(d_out_each, 'expert', split_axis=0, concat_axis=1, tiled=T...]
    another operation x0 -> x1, local copies, waits for them, and re-layouts: none -> 4.33 us  [on_device(): reached = jnp.stack(oldest * [trunk])]
  transfers between devices with their start and end apart: 6 -> 5, of which waited for: 5 -> 3; matrix products, arithmetic and copies ran while one was open for 25% -> 15% of each run, Pallas kernels for 0% -> 0%
where the time goes in v1:
time: 291 us
  waiting for transfers between devices  170 us (58%)
  matrix products  60.7 us (21%)
  blocking collectives  21.6 us (7%)
  between operations  14.2 us (5%)
  starting transfers between devices  11.7 us (4%)
  local copies, waits for them, and re-layouts  9.95 us (3%)
  other arithmetic  2.92 us (1%)
    all_to_all x1, waiting for transfers between devices, on_device(): fresh = lax.all_to_all(reached, ('dp', 'expert'), 0, 0)  163 us
    dot_general x1, matrix products, on_device(): pre = jnp.dot(rows_all, first, preferred_element_type=F32)  20.2 us
    dot_general x1, matrix products, on_device(): lax.dot_general(d_pre_here, first, (((1,), (1,)), ((), ())), preferred_el...  12.9 us
    all_to_all x1, blocking collectives, on_device(): lax.all_to_all(d_out_each, 'expert', split_axis=0, concat_axis=1, tiled=T...  11.4 us
    dot_general x1, matrix products, on_device(): lax.dot_general(d_output_all, second, (((1,), (1,)), ((), ())), preferred...  10.8 us
    all_to_all x1, blocking collectives, on_device(): lax.all_to_all(gate_here.T[None], 'expert', split_axis=1, concat_axis=0,...  10.2 us
    dot_general x1, matrix products, on_device(): lax.dot_general(columns, d_pre, (((0,), (0,)), ((), ())), preferred_eleme...  7.99 us
  transfers between devices with their start and end apart: 5, of which 3 were waited for; matrix products, arithmetic and copies ran while one was open for 15% of the time, Pallas kernels for 0%

profile of v1, /device:TPU:0, one launch (start us, length us, event | category | flops | bytes accessed | tf_op | source)
XLA Modules:
  0.0 291.0 jit_solution(3029622097694692427)
XLA Ops:
  7.2 0.0 copy-start
  7.2 0.9 copy.28
  8.1 10.2 %all_to_all.47 = bf16[1,192,8]{2,0,1:T(2,128)(2,1)S(1)} all-to-all(bf16[1,192,8]{2,0,1:T(2,128)(2,1)S(1)} %copy.28), channel_id=1, replica_groups=mesh['expert'=8,'dp'=4] {'expert'}, dimensions={1} | all-to-all | bytes 6144 | tf_op jit(solution)/shard_map/all_to_all | solution.py:23
  18.3 0.1 copy.29
  18.3 0.1 all_to_all.18
  18.4 0.1 copy.32
  18.5 0.0 copy-done
  18.6 0.2 fusion.19
  18.8 0.2 copy.33
  19.0 11.4 %all_to_all.48 = bf16[8,24,1024]{2,1,0:T(8,128)(2,1)} all-to-all(bf16[8,24,1024]{2,1,0:T(8,128)(2,1)S(1)} %copy.33), channel_id=1, replica_groups=mesh['expert'=8,'dp'=4] {'expert'}, dimensions={0} | all-to-all | bytes 786432 | tf_op jit(solution)/shard_map/all_to_all | solution.py:29
  30.4 4.3 %stack.2 = bf16[32,24,4096]{2,1,0:T(8,128)(2,1)} broadcast(bf16[24,4096]{1,0:T(8,128)(2,1)} %param.5), dimensions={1,2} | broadcast | bytes 6488064 | tf_op jit(solution)/shard_map/stack | solution.py:20
  34.8 4.1 %all-to-all-start = ((bf16[32,24,4096]{2,1,0:T(8,128)(2,1)}), bf16[32,24,4096]{2,1,0:T(8,128)(2,1)}, u32[]{:S(2)}, u32[]{:S(2)}) async-start(bf16[32,24,4096]{2,1,0:T(8,128)(2,1)} %stack.2), calls=%async_computation | async-start | bytes 12582912 | tf_op jit(solution)/shard_map/all_to_all | solution.py:21
  38.9 0.0 all-gather.2.cloned.1.call-start
  38.9 0.7 all-gather.2.cloned.1.call-update
  39.6 0.0 reduce-scatter.2.cloned.1.call-start
  39.6 163.3 %all-to-all-done = bf16[32,24,4096]{2,1,0:T(8,128)(2,1)} async-done(((bf16[32,24,4096]{2,1,0:T(8,128)(2,1)}), bf16[32,24,4096]{2,1,0:T(8,128)(2,1)}, u32[]{:S(2)}, u32[]{:S(2)}) %all-to-all-start) | async-done | bytes 6291488 | tf_op jit(solution)/shard_map/all_to_all | solution.py:21
  203.0 20.2 %fusion.2 = f32[768,2048]{1,0:T(8,128)} fusion(bf16[768,4096]{1,0:T(8,128)(2,1)} %bitcast, bf16[1,4096,2048]{2,1,0:T(8,128)(2,1)} %param.6), kind=kOutput, calls=%fused_computation.2 | convolution fusion | flops 12884901888 | bytes 29360128 | tf_op jit(solution)/shard_map/dot_general | solution.py:31
  223.2 0.0 all-gather.2.cloned.1.call-done
  223.2 10.8 %multiply_convert_fusion = bf16[768,2048]{1,0:T(8,128)(2,1)} fusion(f32[768,2048]{1,0:T(8,128)} %fusion.2, bf16[768,1024]{1,0:T(8,128)(2,1)} %all-gather.2.cloned.1.call-done, bf16[1,2048,1024]{2,1,0:T(8,128)(2,1)} %param.7), kind=kOutput, calls=%fused_computation.4 | convolution fusion | flops 3235381248 | bytes 15204352 | tf_op jit(solution)/shard_map/dot_general | solution.py:36
  233.9 12.9 %fusion.4 = bf16[192,4096]{1,0:T(8,128)(2,1)} fusion(bf16[1,4096,2048]{2,1,0:T(8,128)(2,1)} %param.6, bf16[768,2048]{1,0:T(8,128)(2,1)} %multiply_convert_fusion, s32[]{:T(128)S(6)} %select_n.10), kind=kOutput, calls=%fused_computation.5 | convolution fusion | flops 3222011904 | bytes 19136516 | tf_op jit(solution)/shard_map/dot_general | solution.py:43
  246.8 0.0 reduce-scatter.2.cloned.1.call-update
  246.8 3.7 %fusion.20 = bf16[1,192,1024]{2,1,0:T(8,128)(2,1)S(1)} fusion(bf16[1,2048,1024]{2,1,0:T(8,128)(2,1)} %param.7, f32[768,2048]{1,0:T(8,128)} %fusion.2, s32[]{:T(128)S(6)} %select_n.10), kind=kOutput, calls=%fused_computation.21 | convolution fusion | flops 807469056 | bytes 6160388 | tf_op jit(solution)/shard_map/dot_general | solution.py:34
  250.5 0.6 copy.43
  251.1 0.5 broadcast.11
  251.6 2.9 %reduce = bf16[192,1024]{1,0:T(8,128)(2,1)S(1)} reduce(bf16[192,1,1024]{2,1,0:T(2,128)(2,1)S(1)} %bitcast.57, bf16[]{:T(256)} %broadcast.11), dimensions={1}, to_apply=%bitcast.56.reduce_sub_computation | reduce | bytes 786434
  254.6 1.2 reshape.30
  255.8 3.5 %all-to-all-start.1 = ((bf16[8,2,12288]{2,1,0:T(2,128)(2,1)}), bf16[8,2,12288]{2,1,0:T(2,128)(2,1)S(1)}, u32[]{:S(2)}, u32[]{:S(2)}) async-start(bf16[8,2,12288]{2,1,0:T(2,128)(2,1)} %reshape.30), calls=%async_computation.1 | async-start | bytes 786432 | tf_op jit(solution)/shard_map/all_to_all | solution.py:35
  259.3 0.0 copy-start.1
  259.3 8.0 %convert_bitcast_fusion = bf16[1,1024,2048]{2,1,0:T(8,128)(2,1)} fusion(bf16[768,2048]{1,0:T(8,128)(2,1)} %multiply_convert_fusion, bf16[768,4096]{1,0:T(8,128)(2,1)} %bitcast, s32[]{:T(128)S(6)} %select_n.11), kind=kOutput, calls=%fused_computation.10 | convolution fusion | flops 3223322624 | bytes 8912900 | tf_op jit(solution)/shard_map/dot_general | solution.py:59
  267.3 0.0 copy-done.1
  267.3 3.5 %fusion.14 = bf16[1,512,1024]{2,1,0:T(8,128)(2,1)} fusion(bf16[768,1024]{1,0:T(8,128)(2,1)S(1)} %copy-done.1, f32[768,2048]{1,0:T(8,128)} %fusion.2, s32[]{:T(128)S(6)} %select_n.12), kind=kOutput, calls=%fused_computation.15 | convolution fusion | flops 807796736 | bytes 4194308 | tf_op jit(solution)/shard_map/dot_general | solution.py:64
  270.7 0.0 all-to-all-done.1
  270.7 0.4 reshape.31
  271.1 0.1 copy.37
  271.2 0.4 fusion.23
  271.6 0.7 copy.35
  272.3 4.1 %all-to-all-start.4 = ((bf16[8,24,8]{1,2,0:T(8,128)(2,1)}), bf16[8,24,8]{1,2,0:T(8,128)(2,1)S(1)}, u32[]{:S(2)}, u32[]{:S(2)}) async-start(bf16[8,24,8]{1,2,0:T(8,128)(2,1)} %copy.35), calls=%async_computation.5 | async-start | bytes 32768 | tf_op jit(solution)/shard_map/all_to_all | solution.py:56
  276.4 1.1 fusion.18
  277.6 3.7 %all-to-all-done.4 = bf16[8,24,8]{1,2,0:T(8,128)(2,1)S(1)} async-done(((bf16[8,24,8]{1,2,0:T(8,128)(2,1)}), bf16[8,24,8]{1,2,0:T(8,128)(2,1)S(1)}, u32[]{:S(2)}, u32[]{:S(2)}) %all-to-all-start.4) | async-done | bytes 3104 | tf_op jit(solution)/shard_map/all_to_all | solution.py:56
  281.3 0.7 squeeze.19
  282.0 2.2 reduce-scatter.2.cloned.1.call-done
  (1 shorter events, 0.0 us)
Async XLA Ops:
  7.2 11.4 %copy-start = (bf16[24,8,1024]{2,1,0:T(8,128)(2,1)S(1)}, bf16[24,8,1024]{2,1,0:T(8,128)(2,1)}, u32[]{:S(2)}) copy-start(bf16[24,8,1024]{2,1,0:T(8,128)(2,1)} %param.9) | copy-start | bytes 1179652
  34.8 168.2 %all-to-all-start = ((bf16[32,24,4096]{2,1,0:T(8,128)(2,1)}), bf16[32,24,4096]{2,1,0:T(8,128)(2,1)}, u32[]{:S(2)}, u32[]{:S(2)}) async-start(bf16[32,24,4096]{2,1,0:T(8,128)(2,1)} %stack.2), calls=%async_computation | async-start | bytes 12582912 | tf_op jit(solution)/shard_map/all_to_all | solution.py:21
  38.9 184.3 %all-gather.2.cloned.1.call-start = ((), (), s32[]{:S(2)}) async-start(), calls=%async_computation.6 | async-start | bytes 1966080 | tf_op jit(solution)/shard_map/all_gather | solution.py:30
  39.6 244.6 %reduce-scatter.2.cloned.1.call-start = ((), (), s32[]{:S(2)}) async-start(), calls=%async_computation.7 | async-start | bytes 1769472 | tf_op jit(solution)/shard_map/reduce_scatter | solution.py:42
  255.8 14.9 %all-to-all-start.1 = ((bf16[8,2,12288]{2,1,0:T(2,128)(2,1)}), bf16[8,2,12288]{2,1,0:T(2,128)(2,1)S(1)}, u32[]{:S(2)}, u32[]{:S(2)}) async-start(bf16[8,2,12288]{2,1,0:T(2,128)(2,1)} %reshape.30), calls=%async_computation.1 | async-start | bytes 786432 | tf_op jit(solution)/shard_map/all_to_all | solution.py:35
  259.3 8.0 %copy-start.1 = (bf16[768,1024]{1,0:T(8,128)(2,1)S(1)}, bf16[768,1024]{1,0:T(8,128)(2,1)}, u32[]{:S(2)}) copy-start(bf16[768,1024]{1,0:T(8,128)(2,1)} %all-gather.2.cloned.1.call-done) | copy-start | bytes 4718596
  272.3 9.0 %all-to-all-start.4 = ((bf16[8,24,8]{1,2,0:T(8,128)(2,1)}), bf16[8,24,8]{1,2,0:T(8,128)(2,1)S(1)}, u32[]{:S(2)}, u32[]{:S(2)}) async-start(bf16[8,24,8]{1,2,0:T(8,128)(2,1)} %copy.35), calls=%async_computation.5 | async-start | bytes 32768 | tf_op jit(solution)/shard_map/all_to_all | solution.py:56
Sparse Core Ops, SparseCore 0:
  41.2 76.1 all-gather.1
  247.0 37.1 reduce-scatter.1
